TPU v7x, 256 devices: a whole 4x4x8 slice. The times are simulated.
256 devices in a mesh: chan: 32 (over x, z), win: 8 (over y, core).
Axes of the slice: x: 4, y: 4, z: 8, core: 2. Of those that a mesh axis runs over, the one named last changes fastest.
Arguments:
- spectra: bfloat16 [2, 16, 2048, 1024], P(None, 'win', 'chan'), may hold values from -200 to 200
- pair_blocks: int32 [256, 2], P(('chan', 'win')), may hold values from 0 to 31, as said below
Outputs:
- stacks: float32 [256, 64, 64, 256], P(('chan', 'win'))
Inputs may be any that keep to these rules, and one draw needn't show every extreme that they name: `pair_blocks`: row p belongs to channel block c = p // 8. The 8 rows of c hold, in a drawn order and each in a drawn orientation, the pairs of blocks c - d // 2 and c - d // 2 + d for d = 0 to 7, block numbers taken modulo 32; so every pair of blocks at cyclic distance below 8 appears exactly once in all.
All inputs are finite; a program needn't handle non-finite values.
Results may differ from a plain program's by a relative error of at most 0.0032.
Values may be sent and summed in bfloat16 or wider, within the bound.
No kernel may reach another device: no remote copies, remote signals or barrier semaphores. Data moves between devices by JAX's collectives and lax.ppermute only.
A program may use at most 256 MiB of HBM per device.

v0:
```python
import math
import jax
import jax.numpy as jnp
from jax import lax
from jax.sharding import PartitionSpec as P

NLAG = 256
HALF_BAND = 64
eps = 1e-05
first_bin = 60.0
samples = 15000.0


def shifted(block, axis, distance):
    devices = range(lax.axis_size(axis))
    route = [((i - distance) % len(devices), i) for i in devices]
    return lax.ppermute(block, axis, route)


def smoothing(length_bins, half_width):
    indices = jnp.arange(length_bins, dtype=jnp.int32)
    return (jnp.abs(indices[:, None] - indices[None, :]) <= half_width).astype(jnp.float32)


def whiten(spectra):
    length_bins = spectra.shape[-1]
    real_part = spectra[0].astype(jnp.float32)
    imag_part = spectra[1].astype(jnp.float32)
    powers = real_part * real_part + imag_part * imag_part
    smoother = smoothing(length_bins, HALF_BAND)
    counts = jnp.sum(smoother, axis=0)
    rows_flat = powers.reshape(-1, length_bins)
    smooth = jnp.dot(rows_flat, smoother, precision=lax.Precision.HIGHEST) / counts
    factor = lax.rsqrt(smooth + eps).reshape(powers.shape)
    return jnp.stack([real_part * factor, imag_part * factor]).astype(jnp.bfloat16)


def make_table(length_bins):
    bin_freq = first_bin + jnp.arange(length_bins, dtype=jnp.float32)
    lag_steps = jnp.arange(NLAG, dtype=jnp.float32) - NLAG // 2
    angles = 2.0 * math.pi / samples * bin_freq[:, None] * lag_steps[None, :]
    return jnp.concatenate([jnp.cos(angles), -jnp.sin(angles)], axis=0).astype(jnp.bfloat16)


def cross_spectrum(leading, trailing):
    left_rows = jnp.concatenate([leading[0], leading[1]], axis=0)
    real_rows = jnp.concatenate([trailing[0], trailing[1]], axis=0)
    imag_rows = jnp.concatenate([-trailing[1], trailing[0]], axis=0)
    real_sum = jnp.einsum("wif,wjf->fij", left_rows, real_rows, preferred_element_type=jnp.float32)
    imag_sum = jnp.einsum("wif,wjf->fij", left_rows, imag_rows, preferred_element_type=jnp.float32)
    return jnp.concatenate([real_sum.astype(jnp.bfloat16), imag_sum.astype(jnp.bfloat16)], axis=0)


def per_device(spectra, pair_blocks):
    whitened = whiten(spectra)
    block_size = spectra.shape[2]
    length_bins = spectra.shape[3]
    centre = lax.axis_index("chan")
    block_count = lax.axis_size("chan")
    reach = pair_blocks.shape[0] * lax.axis_size("win") // 2
    offsets = range(1 - reach, reach + 1)
    gathered = lax.all_gather(whitened, "win", axis=1, tiled=True)
    nearby = jnp.stack(
        [gathered if offset == 0 else shifted(gathered, "chan", -offset) for offset in offsets]
    )
    window_total = nearby.shape[2]
    lag_table = make_table(length_bins)
    scaling = 1.0 / math.sqrt(window_total * length_bins)
    base_block = centre - (reach - 1)

    def correlate(pair_row):
        first_slot = jnp.mod(pair_row[0] - base_block, block_count)
        second_slot = jnp.mod(pair_row[1] - base_block, block_count)
        leading = lax.dynamic_index_in_dim(nearby, first_slot, 0, keepdims=False)
        trailing = lax.dynamic_index_in_dim(nearby, second_slot, 0, keepdims=False)
        cross = cross_spectrum(leading, trailing).reshape(2 * length_bins, block_size * block_size)
        result = lax.dot_general(
            cross, lag_table, (((0,), (0,)), ((), ())), preferred_element_type=jnp.float32
        )
        return result.reshape(block_size, block_size, NLAG) * scaling

    return lax.map(correlate, pair_blocks)


def solution(mesh):
    in_specs = (P(None, "win", "chan", None), P(("chan", "win"), None))
    out_specs = P(("chan", "win"), None, None, None)
    return jax.shard_map(
        per_device, mesh=mesh, in_specs=in_specs, out_specs=out_specs, check_vma=False
    )
```

profile of v0, /device:TPU:6, one launch (start us, length us, event | category | flops | bytes accessed | tf_op | source)
XLA Modules:
  0.0 975.5 jit_solution(2766177840453865730)
XLA Ops:
  11.1 37.7 %all-gather.2.cloned.1.call-done = bf16[2,16,64,1024]{3,2,0,1:T(8,128)(2,1)} async-done(((bf16[2,2,64,1024]{3,2,0,1:T(8,128)(2,1)}), bf16[2,16,64,1024]{3,2,0,1:T(8,128)(2,1)}) %all-gather.2.cloned.1.call-update) | async-done | bytes 4194320 | tf_op jit(solution)/shard_map/all_gather | solution.py:62
  65.1 266.4 %collective-permute-done = bf16[2,16,64,1024]{3,2,1,0:T(8,128)(2,1)} collective-permute-done((bf16[2,16,64,1024]{3,2,1,0:T(8,128)(2,1)}, bf16[2,16,64,1024]{3,2,1,0:T(8,128)(2,1)}, u32[]{:S(2)}, u32[]{:S(2)}) %collective-permute-start) | collective-permute-done | bytes 4194336 | tf_op jit(solution)/shard_map/ppermute | solution.py:17
  341.2 11.0 %copy.38 = bf16[2,16,64,1024]{2,1,3,0:T(8,128)(2,1)} copy(bf16[2,16,64,1024]{3,2,0,1:T(8,128)(2,1)} %all-gather.2.cloned.1.call-done) | data formatting | bytes 8388608 | tf_op jit(solution)/shard_map/all_gather | solution.py:62
  352.2 10.9 %copy.33 = bf16[2,16,64,1024]{2,1,3,0:T(8,128)(2,1)} copy(bf16[2,16,64,1024]{3,2,1,0:T(8,128)(2,1)} %collective-permute-done) | data formatting | bytes 8388608 | tf_op jit(solution)/shard_map/ppermute | solution.py:17
  363.1 148.6 %collective-permute-done.1 = bf16[2,16,64,1024]{3,2,1,0:T(8,128)(2,1)} collective-permute-done((bf16[2,16,64,1024]{3,2,1,0:T(8,128)(2,1)}, bf16[2,16,64,1024]{3,2,1,0:T(8,128)(2,1)}, u32[]{:S(2)}, u32[]{:S(2)}) %collective-permute-start.1) | collective-permute-done | bytes 4194336 | tf_op jit(solution)/shard_map/ppermute | solution.py:17
  516.3 10.9 %copy.35 = bf16[2,16,64,1024]{2,1,3,0:T(8,128)(2,1)} copy(bf16[2,16,64,1024]{3,2,1,0:T(8,128)(2,1)} %collective-permute-done.1) | data formatting | bytes 8388608 | tf_op jit(solution)/shard_map/ppermute | solution.py:17
  527.2 74.2 %collective-permute-done.2 = bf16[2,16,64,1024]{3,2,1,0:T(8,128)(2,1)} collective-permute-done((bf16[2,16,64,1024]{3,2,1,0:T(8,128)(2,1)}, bf16[2,16,64,1024]{3,2,1,0:T(8,128)(2,1)}, u32[]{:S(2)}, u32[]{:S(2)}) %collective-permute-start.2) | collective-permute-done | bytes 4194336 | tf_op jit(solution)/shard_map/ppermute | solution.py:17
  601.4 10.9 %copy.37 = bf16[2,16,64,1024]{2,1,3,0:T(8,128)(2,1)} copy(bf16[2,16,64,1024]{3,2,1,0:T(8,128)(2,1)} %collective-permute-done.2) | data formatting | bytes 8388608 | tf_op jit(solution)/shard_map/ppermute | solution.py:17
  612.3 10.9 %copy.40 = bf16[2,16,64,1024]{2,1,3,0:T(8,128)(2,1)} copy(bf16[2,16,64,1024]{3,2,1,0:T(8,128)(2,1)} %collective-permute-done.3) | data formatting | bytes 8388608 | tf_op jit(solution)/shard_map/ppermute | solution.py:17
  623.3 10.9 %copy.42 = bf16[2,16,64,1024]{2,1,3,0:T(8,128)(2,1)} copy(bf16[2,16,64,1024]{3,2,1,0:T(8,128)(2,1)} %collective-permute-done.4) | data formatting | bytes 8388608 | tf_op jit(solution)/shard_map/ppermute | solution.py:17
  634.2 8.0 bitcast_dynamic-update-slice_fusion.7
  642.2 8.0 bitcast_dynamic-update-slice_fusion.6
  650.2 135.4 %collective-permute-done.5 = bf16[2,16,64,1024]{3,2,1,0:T(8,128)(2,1)} collective-permute-done((bf16[2,16,64,1024]{3,2,1,0:T(8,128)(2,1)}, bf16[2,16,64,1024]{3,2,1,0:T(8,128)(2,1)}, u32[]{:S(2)}, u32[]{:S(2)}) %collective-permute-start.5) | collective-permute-done | bytes 4194336 | tf_op jit(solution)/shard_map/ppermute | solution.py:17
  785.6 11.0 %copy.44 = bf16[2,16,64,1024]{2,1,3,0:T(8,128)(2,1)} copy(bf16[2,16,64,1024]{3,2,1,0:T(8,128)(2,1)} %collective-permute-done.5) | data formatting | bytes 8388608 | tf_op jit(solution)/shard_map/ppermute | solution.py:17
  796.7 8.0 bitcast_dynamic-update-slice_fusion.5
  804.7 8.0 bitcast_dynamic-update-slice_fusion.4
  836.9 10.9 %copy.46 = bf16[2,16,64,1024]{2,1,3,0:T(8,128)(2,1)} copy(bf16[2,16,64,1024]{3,2,1,0:T(8,128)(2,1)} %collective-permute-done.6) | data formatting | bytes 8388608 | tf_op jit(solution)/shard_map/ppermute | solution.py:17
  847.8 8.0 bitcast_dynamic-update-slice_fusion
  860.8 8.8 dynamic-slice_bitcast_fusion.3
  869.7 15.6 %convolution_convert_fusion = bf16[1024,64,64]{2,1,0:T(8,128)(2,1)} fusion(bf16[16,64,1024]{1,0,2:T(8,128)(2,1)} %get-tuple-element.24, bf16[16,64,1024]{1,0,2:T(8,128)(2,1)} %get-tuple-element.15, bf16[16,64,1024]{1,0,2:T(8,128)(2,1)} %get-tuple-element.26, bf16[16,64,1024]{1,0,2:T(8,128)(2,1)} %get-tuple-element.17), kind=kOutput, calls=%fused_computation.3 | convolution fusion | flops 289406976 | bytes 16777216 | tf_op jit(solution)/shard_map/while/body/eval_jaxpr/wif,wjf->fij/dot_general | solution.py:50
  885.3 13.7 %convolution_convert_fusion.1 = bf16[1024,64,64]{2,1,0:T(8,128)(2,1)} fusion(bf16[16,64,1024]{1,0,2:T(8,128)(2,1)S(1)} %get-tuple-element.16, bf16[16,64,1024]{1,0,2:T(8,128)(2,1)} %get-tuple-element.24, bf16[16,64,1024]{1,0,2:T(8,128)(2,1)} %get-tuple-element.26, bf16[16,64,1024]{1,0,2:T(8,128)(2,1)} %get-tuple-element.17), kind=kOutput, calls=%fused_computation.4 | convolution fusion | flops 289406976 | bytes 16777216 | tf_op jit(solution)/shard_map/while/body/eval_jaxpr/wif,wjf->fij/dot_general | solution.py:49
  899.0 22.7 %pad_maximum_fusion = bf16[2048,64,64]{2,1,0:T(8,128)(2,1)} fusion(bf16[1024,64,64]{2,1,0:T(8,128)(2,1)} %convolution_convert_fusion, bf16[1024,64,64]{2,1,0:T(8,128)(2,1)} %convolution_convert_fusion.1), kind=kLoop, calls=%fused_computation | loop fusion | flops 8388608 | bytes 33554432 | tf_op jit(solution)/shard_map/while/body/eval_jaxpr/concatenate | solution.py:51
  921.7 35.5 %copy.47 = bf16[2048,64,64]{0,2,1:T(8,128)(2,1)} copy(bf16[2048,64,64]{2,1,0:T(8,128)(2,1)} %pad_maximum_fusion) | data formatting | bytes 33554432 | tf_op jit(solution)/shard_map/while/body/eval_jaxpr/concatenate | solution.py:51
  957.2 11.3 %multiply_bitcast_fusion = f32[1,64,64,256]{3,2,1,0:T(8,128)} fusion(bf16[2048,64,64]{0,2,1:T(8,128)(2,1)} %copy.47, bf16[1024,256]{1,0:T(8,128)(2,1)S(1)} %get-tuple-element.31, bf16[1024,256]{1,0:T(8,128)(2,1)S(1)} %get-tuple-element.30), kind=kOutput, calls=%fused_computation.24 | convolution fusion | flops 4298113024 | bytes 22020096 | tf_op jit(solution)/shard_map/while/body/eval_jaxpr/dot_general | solution.py:77
  (29 shorter events, 62.9 us)
Async XLA Ops:
  6.5 42.3 %all-gather.2.cloned.1.call-start = ((), (), s32[]{:S(2)}) async-start(), calls=%async_computation | async-start | bytes 4718592 | tf_op jit(solution)/shard_map/all_gather | solution.py:62
  7.9 327.1 %copy-start = (s32[1,2]{1,0:T(1,128)S(1)}, s32[1,2]{1,0:T(1,128)}, u32[]{:S(2)}) copy-start(s32[1,2]{1,0:T(1,128)} %param.3) | copy-start | bytes 28
  53.7 277.8 %collective-permute-start = (bf16[2,16,64,1024]{3,2,1,0:T(8,128)(2,1)}, bf16[2,16,64,1024]{3,2,1,0:T(8,128)(2,1)}, u32[]{:S(2)}, u32[]{:S(2)}) collective-permute-start(bf16[2,16,64,1024]{3,2,1,0:T(8,128)(2,1)} %copy.32), channel_id=1, source_target_pairs={{232,0},{240,8},{248,16},{0,24},{8,32},{16,40},{24,48},{32,56},{40... | collective-permute-start | bytes 12582920 | tf_op jit(solution)/shard_map/ppermute | solution.py:17
  57.3 454.4 %collective-permute-start.1 = (bf16[2,16,64,1024]{3,2,1,0:T(8,128)(2,1)}, bf16[2,16,64,1024]{3,2,1,0:T(8,128)(2,1)}, u32[]{:S(2)}, u32[]{:S(2)}) collective-permute-start(bf16[2,16,64,1024]{3,2,1,0:T(8,128)(2,1)} %copy.32), channel_id=1, source_target_pairs={{240,0},{248,8},{0,16},{8,24},{16,32},{24,40},{32,48},{40,56},{48,... | collective-permute-start | bytes 12582920 | tf_op jit(solution)/shard_map/ppermute | solution.py:17
  60.1 541.3 %collective-permute-start.2 = (bf16[2,16,64,1024]{3,2,1,0:T(8,128)(2,1)}, bf16[2,16,64,1024]{3,2,1,0:T(8,128)(2,1)}, u32[]{:S(2)}, u32[]{:S(2)}) collective-permute-start(bf16[2,16,64,1024]{3,2,1,0:T(8,128)(2,1)} %copy.32), channel_id=1, source_target_pairs={{248,0},{0,8},{8,16},{16,24},{24,32},{32,40},{40,48},{48,56},{56,6... | collective-permute-start | bytes 12582920 | tf_op jit(solution)/shard_map/ppermute | solution.py:17
  60.8 551.5 %collective-permute-start.3 = (bf16[2,16,64,1024]{3,2,1,0:T(8,128)(2,1)}, bf16[2,16,64,1024]{3,2,1,0:T(8,128)(2,1)}, u32[]{:S(2)}, u32[]{:S(2)}) collective-permute-start(bf16[2,16,64,1024]{3,2,1,0:T(8,128)(2,1)} %copy.32), channel_id=1, source_target_pairs={{8,0},{16,8},{24,16},{32,24},{40,32},{48,40},{56,48},{64,56},{72,6... | collective-permute-start | bytes 12582920 | tf_op jit(solution)/shard_map/ppermute | solution.py:17
  64.3 559.0 %collective-permute-start.4 = (bf16[2,16,64,1024]{3,2,1,0:T(8,128)(2,1)}, bf16[2,16,64,1024]{3,2,1,0:T(8,128)(2,1)}, u32[]{:S(2)}, u32[]{:S(2)}) collective-permute-start(bf16[2,16,64,1024]{3,2,1,0:T(8,128)(2,1)} %copy.32), channel_id=1, source_target_pairs={{16,0},{24,8},{32,16},{40,24},{48,32},{56,40},{64,48},{72,56},{80,... | collective-permute-start | bytes 12582920 | tf_op jit(solution)/shard_map/ppermute | solution.py:17
  331.5 454.1 %collective-permute-start.5 = (bf16[2,16,64,1024]{3,2,1,0:T(8,128)(2,1)}, bf16[2,16,64,1024]{3,2,1,0:T(8,128)(2,1)}, u32[]{:S(2)}, u32[]{:S(2)}) collective-permute-start(bf16[2,16,64,1024]{3,2,1,0:T(8,128)(2,1)} %copy.32), channel_id=1, source_target_pairs={{24,0},{32,8},{40,16},{48,24},{56,32},{64,40},{72,48},{80,56},{88,... | collective-permute-start | bytes 12582920 | tf_op jit(solution)/shard_map/ppermute | solution.py:17
  511.7 325.2 %collective-permute-start.6 = (bf16[2,16,64,1024]{3,2,1,0:T(8,128)(2,1)}, bf16[2,16,64,1024]{3,2,1,0:T(8,128)(2,1)}, u32[]{:S(2)}, u32[]{:S(2)}) collective-permute-start(bf16[2,16,64,1024]{3,2,1,0:T(8,128)(2,1)} %copy.32), channel_id=1, source_target_pairs={{32,0},{40,8},{48,16},{56,24},{64,32},{72,40},{80,48},{88,56},{96,... | collective-permute-start | bytes 12582920 | tf_op jit(solution)/shard_map/ppermute | solution.py:17
Sparse Core Ops, SparseCore 0:
  11.2 37.5 all-gather.1
where the time goes:
time: 986 us; the launch traced here: 976 us
  waiting for transfers between devices  662 us (67%)
  local copies, waits for them, and re-layouts  202 us (20%)
  matrix products  41.7 us (4%)
  other arithmetic  34.5 us (3%)
  starting transfers between devices  19.5 us (2%)
  between operations  14.9 us (2%)
    ppermute x7, waiting for transfers between devices, shifted(): return lax.ppermute(block, axis, route)  625 us
    ppermute x7, local copies, waits for them, and re-layouts, shifted(): return lax.ppermute(block, axis, route)  76.5 us
    unnamed x9, local copies, waits for them, and re-layouts  56.3 us
    all_gather x1, waiting for transfers between devices, per_device(): gathered = lax.all_gather(whitened, 'win', axis=1, tiled=True)  37.7 us
    concatenate x1, local copies, waits for them, and re-layouts, cross_spectrum(): jnp.concatenate([real_sum.astype(jnp.bfloat16), imag_sum.astype(jnp.bfloa...  35.5 us
    concatenate x1, other arithmetic, cross_spectrum(): jnp.concatenate([real_sum.astype(jnp.bfloat16), imag_sum.astype(jnp.bfloa...  22.7 us
  transfers between devices with their start and end apart: 8, of which 5 were waited for; matrix products, arithmetic and copies ran while one was open for 14% of the time, Pallas kernels for 0%

commit v1 on v0

--- a/solution.py
+++ b/solution.py
@@ -59,7 +59,10 @@
     block_count = lax.axis_size("chan")
     reach = pair_blocks.shape[0] * lax.axis_size("win") // 2
     offsets = range(1 - reach, reach + 1)
-    gathered = lax.all_gather(whitened, "win", axis=1, tiled=True)
+    n_dev = lax.axis_size("win")
+    pieces = jnp.stack([whitened for _ in range(n_dev)])
+    pieces = lax.all_to_all(pieces, "win", split_axis=0, concat_axis=0)
+    gathered = jnp.concatenate(pieces, axis=1)
     nearby = jnp.stack(
         [gathered if offset == 0 else shifted(gathered, "chan", -offset) for offset in offsets]
     )

time: 986 us -> 1020 us (1.034)
  the two profiles are of different devices: /device:TPU:6 before, /device:TPU:70 now
where the time goes in v1:
time: 1020 us; the launch traced here: 1010 us
  waiting for transfers between devices  645 us (63%)
  local copies, waits for them, and re-layouts  211 us (21%)
  blocking collectives  54.6 us (5%)
  matrix products  41.8 us (4%)
  other arithmetic  34.6 us (3%)
  starting transfers between devices  16.4 us (2%)
    ppermute x7, waiting for transfers between devices, shifted(): return lax.ppermute(block, axis, route)  645 us
    ppermute x7, local copies, waits for them, and re-layouts, shifted(): return lax.ppermute(block, axis, route)  76.6 us
    unnamed x11, local copies, waits for them, and re-layouts  58.2 us
    all_to_all x1, blocking collectives, per_device(): pieces = lax.all_to_all(pieces, 'win', split_axis=0, concat_axis=0)  54.6 us
    concatenate x1, local copies, waits for them, and re-layouts, cross_spectrum(): jnp.concatenate([real_sum.astype(jnp.bfloat16), imag_sum.astype(jnp.bfloa...  35.4 us
    concatenate x1, other arithmetic, cross_spectrum(): jnp.concatenate([real_sum.astype(jnp.bfloat16), imag_sum.astype(jnp.bfloa...  22.7 us
    reshape x1, local copies, waits for them, and re-layouts, per_device(): gathered = jnp.concatenate(pieces, axis=1)  20.6 us
  transfers between devices with their start and end apart: 7, of which 3 were waited for; matrix products, arithmetic and copies ran while one was open for 15% of the time, Pallas kernels for 0%

profile of v1, /device:TPU:70, one launch (start us, length us, event | category | flops | bytes accessed | tf_op | source)
XLA Modules:
  0.0 1005.6 jit_solution(7392559595535675110)
XLA Ops:
  4.2 54.6 %all_to_all.5 = bf16[8,2,2,64,1024]{4,3,2,1,0:T(8,128)(2,1)S(1)} all-to-all(bf16[8,2,2,64,1024]{4,3,2,1,0:T(8,128)(2,1)S(1)} %stack.41), channel_id=1, replica_groups=mesh['chan'=32,'win'=8] {'win'}, dimensions={0} | all-to-all | bytes 8388608 | tf_op jit(solution)/shard_map/all_to_all | solution.py:64
  75.2 263.5 %collective-permute-done = bf16[2,16,64,1024]{3,2,1,0:T(8,128)(2,1)} collective-permute-done((bf16[2,16,64,1024]{3,2,1,0:T(8,128)(2,1)}, bf16[2,16,64,1024]{3,2,1,0:T(8,128)(2,1)}, u32[]{:S(2)}, u32[]{:S(2)}) %collective-permute-start) | collective-permute-done | bytes 4194336 | tf_op jit(solution)/shard_map/ppermute | solution.py:17
  348.9 20.6 %copy.30 = bf16[2,8,2,64,1024]{3,2,1,4,0:T(2,128)(2,1)} copy(bf16[2,8,2,64,1024]{4,3,2,0,1:T(8,128)(2,1)} %bitcast.47) | data formatting | bytes 8388608 | tf_op jit(solution)/shard_map/reshape | solution.py:65
  369.5 10.9 %copy.27 = bf16[2,16,64,1024]{2,1,3,0:T(8,128)(2,1)} copy(bf16[2,16,64,1024]{3,2,1,0:T(8,128)(2,1)} %collective-permute-done) | data formatting | bytes 8388608 | tf_op jit(solution)/shard_map/ppermute | solution.py:17
  380.4 140.5 %collective-permute-done.1 = bf16[2,16,64,1024]{3,2,1,0:T(8,128)(2,1)} collective-permute-done((bf16[2,16,64,1024]{3,2,1,0:T(8,128)(2,1)}, bf16[2,16,64,1024]{3,2,1,0:T(8,128)(2,1)}, u32[]{:S(2)}, u32[]{:S(2)}) %collective-permute-start.1) | collective-permute-done | bytes 4194336 | tf_op jit(solution)/shard_map/ppermute | solution.py:17
  521.4 10.9 %copy.28 = bf16[2,16,64,1024]{2,1,3,0:T(8,128)(2,1)} copy(bf16[2,16,64,1024]{3,2,1,0:T(8,128)(2,1)} %collective-permute-done.1) | data formatting | bytes 8388608 | tf_op jit(solution)/shard_map/ppermute | solution.py:17
  532.3 8.0 bitcast_dynamic-update-slice_fusion.6
  540.3 8.1 bitcast_dynamic-update-slice_fusion.5
  548.4 241.3 %collective-permute-done.2 = bf16[2,16,64,1024]{3,2,1,0:T(8,128)(2,1)} collective-permute-done((bf16[2,16,64,1024]{3,2,1,0:T(8,128)(2,1)}, bf16[2,16,64,1024]{3,2,1,0:T(8,128)(2,1)}, u32[]{:S(2)}, u32[]{:S(2)}) %collective-permute-start.2) | collective-permute-done | bytes 4194336 | tf_op jit(solution)/shard_map/ppermute | solution.py:17
  789.7 10.9 %copy.29 = bf16[2,16,64,1024]{2,1,3,0:T(8,128)(2,1)} copy(bf16[2,16,64,1024]{3,2,1,0:T(8,128)(2,1)} %collective-permute-done.2) | data formatting | bytes 8388608 | tf_op jit(solution)/shard_map/ppermute | solution.py:17
  800.6 10.9 %copy.31 = bf16[2,16,64,1024]{2,1,3,0:T(8,128)(2,1)} copy(bf16[2,16,64,1024]{3,2,1,0:T(8,128)(2,1)} %collective-permute-done.3) | data formatting | bytes 8388608 | tf_op jit(solution)/shard_map/ppermute | solution.py:17
  811.5 10.9 %copy.32 = bf16[2,16,64,1024]{2,1,3,0:T(8,128)(2,1)} copy(bf16[2,16,64,1024]{3,2,1,0:T(8,128)(2,1)} %collective-permute-done.4) | data formatting | bytes 8388608 | tf_op jit(solution)/shard_map/ppermute | solution.py:17
  822.4 11.1 %copy.33 = bf16[2,16,64,1024]{2,1,3,0:T(8,128)(2,1)} copy(bf16[2,16,64,1024]{3,2,1,0:T(8,128)(2,1)} %collective-permute-done.5) | data formatting | bytes 8388608 | tf_op jit(solution)/shard_map/ppermute | solution.py:17
  833.5 8.0 bitcast_dynamic-update-slice_fusion.4
  841.6 8.0 constant_dynamic-update-slice_fusion
  865.7 8.0 bitcast_dynamic-update-slice_fusion.1
  873.7 11.0 %copy.34 = bf16[2,16,64,1024]{2,1,3,0:T(8,128)(2,1)} copy(bf16[2,16,64,1024]{3,2,1,0:T(8,128)(2,1)} %collective-permute-done.6) | data formatting | bytes 8388608 | tf_op jit(solution)/shard_map/ppermute | solution.py:17
  884.7 8.0 bitcast_dynamic-update-slice_fusion
  897.7 8.8 dynamic-slice_bitcast_fusion.3
  906.5 15.7 %convolution_convert_fusion = bf16[1024,64,64]{2,1,0:T(8,128)(2,1)} fusion(bf16[16,64,1024]{1,0,2:T(8,128)(2,1)} %get-tuple-element.24, bf16[16,64,1024]{1,0,2:T(8,128)(2,1)} %get-tuple-element.15, bf16[16,64,1024]{1,0,2:T(8,128)(2,1)} %get-tuple-element.26, bf16[16,64,1024]{1,0,2:T(8,128)(2,1)} %get-tuple-element.17), kind=kOutput, calls=%fused_computation.3 | convolution fusion | flops 289406976 | bytes 16777216 | tf_op jit(solution)/shard_map/while/body/eval_jaxpr/wif,wjf->fij/dot_general | solution.py:50
  922.2 13.8 %convolution_convert_fusion.1 = bf16[1024,64,64]{2,1,0:T(8,128)(2,1)} fusion(bf16[16,64,1024]{1,0,2:T(8,128)(2,1)S(1)} %get-tuple-element.16, bf16[16,64,1024]{1,0,2:T(8,128)(2,1)} %get-tuple-element.24, bf16[16,64,1024]{1,0,2:T(8,128)(2,1)} %get-tuple-element.26, bf16[16,64,1024]{1,0,2:T(8,128)(2,1)} %get-tuple-element.17), kind=kOutput, calls=%fused_computation.4 | convolution fusion | flops 289406976 | bytes 16777216 | tf_op jit(solution)/shard_map/while/body/eval_jaxpr/wif,wjf->fij/dot_general | solution.py:49
  935.9 22.7 %pad_maximum_fusion = bf16[2048,64,64]{2,1,0:T(8,128)(2,1)} fusion(bf16[1024,64,64]{2,1,0:T(8,128)(2,1)} %convolution_convert_fusion, bf16[1024,64,64]{2,1,0:T(8,128)(2,1)} %convolution_convert_fusion.1), kind=kLoop, calls=%fused_computation | loop fusion | flops 8388608 | bytes 33554432 | tf_op jit(solution)/shard_map/while/body/eval_jaxpr/concatenate | solution.py:51
  958.7 35.4 %copy.35 = bf16[2048,64,64]{0,2,1:T(8,128)(2,1)} copy(bf16[2048,64,64]{2,1,0:T(8,128)(2,1)} %pad_maximum_fusion) | data formatting | bytes 33554432 | tf_op jit(solution)/shard_map/while/body/eval_jaxpr/concatenate | solution.py:51
  994.1 11.3 %multiply_bitcast_fusion = f32[1,64,64,256]{3,2,1,0:T(8,128)} fusion(bf16[2048,64,64]{0,2,1:T(8,128)(2,1)} %copy.35, bf16[1024,256]{1,0:T(8,128)(2,1)S(1)} %get-tuple-element.31, bf16[1024,256]{1,0:T(8,128)(2,1)S(1)} %get-tuple-element.30), kind=kOutput, calls=%fused_computation.23 | convolution fusion | flops 4298113024 | bytes 22020096 | tf_op jit(solution)/shard_map/while/body/eval_jaxpr/dot_general | solution.py:80
  (29 shorter events, 50.9 us)
Async XLA Ops:
  4.2 338.5 %copy-start.1 = (s32[1,2]{1,0:T(1,128)S(1)}, s32[1,2]{1,0:T(1,128)}, u32[]{:S(2)}) copy-start(s32[1,2]{1,0:T(1,128)} %param.3) | copy-start | bytes 28
  58.8 2.0 copy-start
  63.2 275.5 %collective-permute-start = (bf16[2,16,64,1024]{3,2,1,0:T(8,128)(2,1)}, bf16[2,16,64,1024]{3,2,1,0:T(8,128)(2,1)}, u32[]{:S(2)}, u32[]{:S(2)}) collective-permute-start(bf16[2,16,64,1024]{3,2,1,0:T(8,128)(2,1)} %bitcast.3), channel_id=1, source_target_pairs={{232,0},{240,8},{248,16},{0,24},{8,32},{16,40},{24,48},{32,56},{40... | collective-permute-start | bytes 12582920 | tf_op jit(solution)/shard_map/ppermute | solution.py:17
  68.2 452.7 %collective-permute-start.1 = (bf16[2,16,64,1024]{3,2,1,0:T(8,128)(2,1)}, bf16[2,16,64,1024]{3,2,1,0:T(8,128)(2,1)}, u32[]{:S(2)}, u32[]{:S(2)}) collective-permute-start(bf16[2,16,64,1024]{3,2,1,0:T(8,128)(2,1)} %bitcast.3), channel_id=1, source_target_pairs={{240,0},{248,8},{0,16},{8,24},{16,32},{24,40},{32,48},{40,56},{48,... | collective-permute-start | bytes 12582920 | tf_op jit(solution)/shard_map/ppermute | solution.py:17
  69.6 720.1 %collective-permute-start.2 = (bf16[2,16,64,1024]{3,2,1,0:T(8,128)(2,1)}, bf16[2,16,64,1024]{3,2,1,0:T(8,128)(2,1)}, u32[]{:S(2)}, u32[]{:S(2)}) collective-permute-start(bf16[2,16,64,1024]{3,2,1,0:T(8,128)(2,1)} %bitcast.3), channel_id=1, source_target_pairs={{248,0},{0,8},{8,16},{16,24},{24,32},{32,40},{40,48},{48,56},{56,6... | collective-permute-start | bytes 12582920 | tf_op jit(solution)/shard_map/ppermute | solution.py:17
  69.6 730.9 %collective-permute-start.3 = (bf16[2,16,64,1024]{3,2,1,0:T(8,128)(2,1)}, bf16[2,16,64,1024]{3,2,1,0:T(8,128)(2,1)}, u32[]{:S(2)}, u32[]{:S(2)}) collective-permute-start(bf16[2,16,64,1024]{3,2,1,0:T(8,128)(2,1)} %bitcast.3), channel_id=1, source_target_pairs={{8,0},{16,8},{24,16},{32,24},{40,32},{48,40},{56,48},{64,56},{72,6... | collective-permute-start | bytes 12582920 | tf_op jit(solution)/shard_map/ppermute | solution.py:17
  71.7 739.9 %collective-permute-start.4 = (bf16[2,16,64,1024]{3,2,1,0:T(8,128)(2,1)}, bf16[2,16,64,1024]{3,2,1,0:T(8,128)(2,1)}, u32[]{:S(2)}, u32[]{:S(2)}) collective-permute-start(bf16[2,16,64,1024]{3,2,1,0:T(8,128)(2,1)} %bitcast.3), channel_id=1, source_target_pairs={{16,0},{24,8},{32,16},{40,24},{48,32},{56,40},{64,48},{72,56},{80,... | collective-permute-start | bytes 12582920 | tf_op jit(solution)/shard_map/ppermute | solution.py:17
  338.7 483.7 %collective-permute-start.5 = (bf16[2,16,64,1024]{3,2,1,0:T(8,128)(2,1)}, bf16[2,16,64,1024]{3,2,1,0:T(8,128)(2,1)}, u32[]{:S(2)}, u32[]{:S(2)}) collective-permute-start(bf16[2,16,64,1024]{3,2,1,0:T(8,128)(2,1)} %bitcast.3), channel_id=1, source_target_pairs={{24,0},{32,8},{40,16},{48,24},{56,32},{64,40},{72,48},{80,56},{88,... | collective-permute-start | bytes 12582920 | tf_op jit(solution)/shard_map/ppermute | solution.py:17
  520.9 352.8 %collective-permute-start.6 = (bf16[2,16,64,1024]{3,2,1,0:T(8,128)(2,1)}, bf16[2,16,64,1024]{3,2,1,0:T(8,128)(2,1)}, u32[]{:S(2)}, u32[]{:S(2)}) collective-permute-start(bf16[2,16,64,1024]{3,2,1,0:T(8,128)(2,1)} %bitcast.3), channel_id=1, source_target_pairs={{32,0},{40,8},{48,16},{56,24},{64,32},{72,40},{80,48},{88,56},{96,... | collective-permute-start | bytes 12582920 | tf_op jit(solution)/shard_map/ppermute | solution.py:17
